TPU v7x, 32 devices: a whole 2x2x4 slice. The times are simulated.
32 devices in a mesh: wide: 4 (over z), narrow: 8 (over y, x, core).
Axes of the slice: x: 2, y: 2, z: 4, core: 2. Of those that a mesh axis runs over, the one named last changes fastest.
Arguments:
- phase_ids: int32 [512, 512, 256], P('wide', 'narrow'), may hold values from 0 to 3
- conduct_table: float32 [4, 3], replicated, may hold values from 0.2 to 5
- gradient: float32 [3], replicated, may hold values from -3 to 3
- start_field: float32 [512, 512, 256], P('wide', 'narrow'), may hold values from -32 to 32
Outputs:
- solution: float32 [512, 512, 256], P('wide', 'narrow')
- residual_next: float32 [512, 512, 256], P('wide', 'narrow')
- new_direction: float32 [512, 512, 256], P('wide', 'narrow')
Inputs may be any that keep to these rules, and one draw needn't show every extreme that they name: `phase_ids`: each voxel's phase indexes a row of conduct_table.
All inputs are finite; a program needn't handle non-finite values.
Results may differ from a plain program's by a relative error of at most 0.0065.
Values sent between devices are 32-bit elements; how exact they have to be, the bound alone decides.
No kernel may reach another device: no remote copies, remote signals or barrier semaphores. Data moves between devices by JAX's collectives and lax.ppermute only.
A program may use at most 256 MiB of HBM per device.

v0:
```python
import jax
import jax.numpy as jnp
from jax import lax
from jax.sharding import PartitionSpec as P

NX = 512
NY = 512
NZ = 256
PHASES = 4
HIGHEST = lax.Precision.HIGHEST
FORWARD_FORMS = ("nyz,mn->myz", "xnz,mn->xmz", "xyn,mn->xym")
INVERSE_FORMS = ("myz,mn->nyz", "xmz,mn->xnz", "xym,mn->xyn")


def extended(shard, sides, width):
    for axis, dim in sides:
        devices, length = (lax.axis_size(axis), shard.shape[dim])
        up = [(i, (i + 1) % devices) for i in range(devices - 1)]
        down = [(j, i) for i, j in up]
        last = lax.slice_in_dim(shard, length - width, length, axis=dim)
        initial = lax.slice_in_dim(shard, 0, width, axis=dim)
        before = lax.ppermute(last, axis, up)
        after = lax.ppermute(initial, axis, down)
        shard = jnp.concatenate([before, shard, after], axis=dim)
    return shard


def cosine_table(length):
    freq_index = jnp.arange(length, dtype=jnp.int32)[:, None]
    cell_index = jnp.arange(length, dtype=jnp.int32)[None, :]
    wrapped = freq_index * (2 * cell_index + 1) % (4 * length)
    angle_rad = wrapped.astype(jnp.float32) * (jnp.pi / (2.0 * length))
    weight = jnp.where(
        freq_index == 0, jnp.sqrt(jnp.float32(1.0 / length)), jnp.sqrt(jnp.float32(2.0 / length))
    )
    return weight * jnp.cos(angle_rad)


def eigen_values(length, index):
    angle_rad = index.astype(jnp.float32) * (jnp.pi / length)
    return 2.0 - 2.0 * jnp.cos(angle_rad)


def green_block(base_cond, index_x, index_y, index_z):
    lowest = eigen_values(NX, jnp.ones((), jnp.int32))
    eigen_sum = lowest + eigen_values(NX, index_x)[:, None, None]
    eigen_sum = eigen_sum + eigen_values(NY, index_y)[None, :, None]
    eigen_sum = eigen_sum + eigen_values(NZ, index_z)[None, None, :]
    zero_mode = (
        (index_x[:, None, None] == 0)
        & (index_y[None, :, None] == 0)
        & (index_z[None, None, :] == 0)
    )
    return jnp.where(zero_mode, jnp.float32(0.0), 1.0 / (base_cond * eigen_sum))


def transform(values, matrix, axis_dim, inverse):
    einsum_form = INVERSE_FORMS[axis_dim] if inverse else FORWARD_FORMS[axis_dim]
    return jnp.einsum(einsum_form, values, matrix, precision=HIGHEST)


def harmonic(lower_side, upper_side):
    return 2.0 * lower_side * upper_side / (lower_side + upper_side)


def conductivities(phase_ids, conduct_table):
    result = []
    for component in range(3):
        summed = jnp.zeros(phase_ids.shape, jnp.float32)
        for member in range(PHASES):
            summed = summed + jnp.where(
                phase_ids == member, conduct_table[member, component], jnp.float32(0.0)
            )
        result.append(summed)
    return result


def pad_depth(values):
    return jnp.pad(values, ((0, 0), (0, 0), (1, 1)))


def apply_padded(field_pad, faces):
    inner_x = field_pad[:, 1:-1, :]
    flux_x = faces[0] * (inner_x[1:] - inner_x[:-1])
    inner_y = field_pad[1:-1, :, :]
    flux_y = faces[1] * (inner_y[:, 1:] - inner_y[:, :-1])
    inner_z = pad_depth(field_pad[1:-1, 1:-1, :])
    flux_z = faces[2] * (inner_z[:, :, 1:] - inner_z[:, :, :-1])
    divergence = flux_x[1:] - flux_x[:-1] + (flux_y[:, 1:] - flux_y[:, :-1])
    divergence = divergence + (flux_z[:, :, 1:] - flux_z[:, :, :-1])
    return -divergence


def precondition(grid_field, tables, base_cond):
    table_x, table_y, table_z = tables
    spectral = transform(grid_field, table_z, 2, False)
    spectral = transform(
        lax.all_to_all(spectral, "narrow", split_axis=2, concat_axis=1, tiled=True),
        table_y,
        1,
        False,
    )
    spectral = transform(
        lax.all_to_all(spectral, "wide", split_axis=1, concat_axis=0, tiled=True), table_x, 0, False
    )
    count_y = spectral.shape[1]
    count_z = spectral.shape[2]
    index_x = jnp.arange(NX, dtype=jnp.int32)
    index_y = lax.axis_index("wide") * count_y + jnp.arange(count_y, dtype=jnp.int32)
    index_z = lax.axis_index("narrow") * count_z + jnp.arange(count_z, dtype=jnp.int32)
    spectral = spectral * green_block(base_cond, index_x, index_y, index_z)
    spectral = transform(spectral, table_x, 0, True)
    spectral = transform(
        lax.all_to_all(spectral, "wide", split_axis=0, concat_axis=1, tiled=True), table_y, 1, True
    )
    return transform(
        lax.all_to_all(spectral, "narrow", split_axis=1, concat_axis=2, tiled=True),
        table_z,
        2,
        True,
    )


def on_device(phase_ids, conduct_table, gradient, start_field):
    cond_x, cond_y, cond_z = conductivities(phase_ids, conduct_table)
    stacked = jnp.stack([start_field, cond_x, cond_y])
    padded = extended(stacked, (("wide", 1), ("narrow", 2)), 1)
    start_pad = padded[0]
    cond_xp = padded[1][:, 1:-1, :]
    cond_yp = padded[2][1:-1, :, :]
    cond_zp = pad_depth(cond_z)
    faces = (
        harmonic(cond_xp[:-1], cond_xp[1:]),
        harmonic(cond_yp[:, :-1], cond_yp[:, 1:]),
        harmonic(cond_zp[:, :, :-1], cond_zp[:, :, 1:]),
    )
    source = gradient[0] * (faces[0][1:] - faces[0][:-1])
    source = source + gradient[1] * (faces[1][:, 1:] - faces[1][:, :-1])
    source = source + gradient[2] * (faces[2][:, :, 1:] - faces[2][:, :, :-1])
    residual = source - apply_padded(start_pad, faces)
    tables = (cosine_table(NX), cosine_table(NY), cosine_table(NZ))
    base_cond = jnp.mean(conduct_table)
    direction = precondition(residual, tables, base_cond)
    direction_pad = extended(direction, (("wide", 0), ("narrow", 1)), 1)
    image_field = apply_padded(direction_pad, faces)
    rz_now = lax.psum(jnp.sum(residual * direction), ("wide", "narrow"))
    curvature = lax.psum(jnp.sum(direction * image_field), ("wide", "narrow"))
    step_alpha = rz_now / curvature
    solution = start_field + step_alpha * direction
    residual_next = residual - step_alpha * image_field
    preconditioned = precondition(residual_next, tables, base_cond)
    rz_next = lax.psum(jnp.sum(residual_next * preconditioned), ("wide", "narrow"))
    new_direction = preconditioned + rz_next / rz_now * direction
    return (solution, residual_next, new_direction)


def solution(mesh):
    placed = (P("wide", "narrow", None), P(), P(), P("wide", "narrow", None))
    return jax.shard_map(
        on_device,
        mesh=mesh,
        in_specs=placed,
        out_specs=(P("wide", "narrow", None), P("wide", "narrow", None), P("wide", "narrow", None)),
        check_vma=False,
    )
```

profile of v0, /device:TPU:0, one launch (start us, length us, event | category | flops | bytes accessed | tf_op | source)
XLA Modules:
  0.0 1928.2 jit_solution(9255614372349274259)
XLA Ops:
  2.4 8.4 copy.155
  10.8 14.0 add_bitcast_fusion.1
  24.8 14.6 select_add_fusion
  59.9 10.3 pad_maximum_fusion
  70.2 11.6 slice_bitcast_fusion.3
  81.7 10.8 slice_bitcast_fusion.1
  98.6 19.2 fusion.4
  117.8 19.0 fusion.8
  136.8 22.0 %fusion.1 = (f32[128,64,257]{2,0,1:T(8,128)}, f32[128,64,257]{2,0,1:T(8,128)}) fusion(f32[128,64,256]{2,0,1:T(8,128)} %slice.296, f32[128,64,256]{2,0,1:T(8,128)} %get-tuple-element.45), kind=kLoop, calls=%fused_computation.8 | loop fusion | flops 12632064 | bytes 33619968 | tf_op jit(solution)/shard_map/mul | solution.py:88
  158.8 41.1 %fusion.14 = f32[128,64,256]{2,0,1:T(8,128)} fusion(f32[128,64,257]{2,0,1:T(8,128)} %get-tuple-element.24, f32[128,65,256]{2,0,1:T(8,128)} %get-tuple-element.22, f32[129,64,256]{2,0,1:T(8,128)} %get-tuple-element.20, f32[128,64,257]{2,0,1:T(8,128)} %get-tuple-element.25, f32[128,65,256]{2,0,1:T(8,128)} %get-tuple-element.23, ...), kind=kLoop, calls=%fused_computation.41 | loop fusion | flops 31457280 | bytes 109051920 | tf_op jit(solution)/shard_map/sub | solution.py:140
  199.9 13.0 fusion.131
  213.0 8.7 copy.87
  221.6 10.1 all-to-all-start
  231.8 94.1 %all-to-all-done = f32[128,64,256]{0,1,2:T(8,128)} async-done(((f32[128,64,256]{0,1,2:T(8,128)}), f32[128,64,256]{0,1,2:T(8,128)}, u32[]{:S(2)}, u32[]{:S(2)}) %all-to-all-start) | async-done | bytes 8388640 | tf_op jit(solution)/shard_map/all_to_all | solution.py:98
  334.1 29.1 %fusion.43 = f32[128,512,32]{0,1,2:T(8,128)S(1)} fusion(f32[128,512,32]{0,2,1:T(8,128)S(1)} %bitcast.111, s32[512]{0:T(512)S(1)} %multiply_add_fusion.2, f32[512]{0:T(512)S(1)} %broadcast_select_fusion), kind=kOutput, calls=%fused_computation.92 | convolution fusion | flops 12888834048 | bytes 16781312 | tf_op jit(solution)/shard_map/xnz,mn->xmz/dot_general | solution.py:59
  363.2 8.3 copy.92
  379.0 179.1 %all-to-all-done.1 = f32[128,512,32]{0,2,1:T(8,128)} async-done(((f32[128,512,32]{0,2,1:T(8,128)}), f32[128,512,32]{0,2,1:T(8,128)}, u32[]{:S(2)}, u32[]{:S(2)}) %all-to-all-start.1) | async-done | bytes 8388640 | tf_op jit(solution)/shard_map/all_to_all | solution.py:104
  558.1 9.9 copy.128
  568.0 22.5 %fusion.62 = f32[512,128,32]{1,0,2:T(8,128)S(1)} fusion(f32[512,128,32]{1,0,2:T(8,128)} %bitcast.109, s32[512]{0:T(512)S(1)} %multiply_add_fusion.2, f32[512]{0:T(512)S(1)} %broadcast_select_fusion), kind=kOutput, calls=%fused_computation.109 | convolution fusion | flops 12888834048 | bytes 16781312 | tf_op jit(solution)/shard_map/nyz,mn->myz/dot_general | solution.py:59
  590.5 20.1 %fusion.27 = f32[512,128,32]{1,0,2:T(8,128)S(1)} fusion(f32[512,128,32]{1,0,2:T(8,128)S(1)} %fusion.62, f32[32]{0:T(128)S(1)} %multiply_subtract_fusion.2, f32[512,128]{1,0:T(8,128)S(1)} %broadcast_add_fusion, f32[]{:T(128)S(6)} %div.25, pred[512,128]{1,0:T(8,128)(4,1)S(1)} %broadcast_and_fusion, pred[32]{0:T(512)(128)(4,1)S(1)} %fusion.157, ...), kind=kOutput, calls=%fused_computation.67 | convolution fusion | flops 12901416960 | bytes 17109156 | tf_op jit(solution)/shard_map/myz,mn->nyz/dot_general | solution.py:59
  615.5 186.7 %all_to_all.144 = f32[512,128,32]{1,2,0:T(8,128)} all-to-all(f32[512,128,32]{1,2,0:T(8,128)S(1)} %copy.96), channel_id=1, replica_groups=mesh['wide'=4,'narrow'=8] {'wide'}, dimensions={0} | all-to-all | bytes 16777216 | tf_op jit(solution)/shard_map/all_to_all | solution.py:114
  802.1 12.2 copy.154
  814.3 10.3 all_to_all.115
  824.6 24.8 %convolution_bitcast_fusion.1 = f32[128,512,32]{0,1,2:T(8,128)S(1)} fusion(f32[128,512,32]{1,0,2:T(8,128)} %all_to_all.115, s32[512]{0:T(512)S(1)} %multiply_add_fusion.2, f32[512]{0:T(512)S(1)} %broadcast_select_fusion), kind=kOutput, calls=%fused_computation.95 | convolution fusion | flops 12888834048 | bytes 16781312 | tf_op jit(solution)/shard_map/xmz,mn->xnz/dot_general | solution.py:59
  854.3 98.0 %all_to_all.145 = f32[128,512,32]{0,2,1:T(8,128)S(1)} all-to-all(f32[128,512,32]{0,2,1:T(8,128)S(1)} %copy.98), channel_id=1, replica_groups=mesh['wide'=4,'narrow'=8] {'narrow'}, dimensions={1} | all-to-all | bytes 16777216 | tf_op jit(solution)/shard_map/all_to_all | solution.py:117
  956.8 18.2 fusion.129
  978.5 10.8 fusion.3
  1008.0 25.2 %multiply_reduce_fusion.1 = (f32[]{:T(128)}, f32[]{:T(128)}, f32[128,64,256]{2,0,1:T(8,128)}) fusion(f32[128,64,256]{2,0,1:T(8,128)S(1)} %fusion.129, f32[128,64,256]{2,0,1:T(8,128)} %fusion.14, f32[128,64,257]{2,0,1:T(8,128)} %fusion.3, f32[128,65,256]{2,0,1:T(8,128)} %fusion.7, f32[129,64,256]{2,0,1:T(8,128)} %fusion.5), kind=kLoop, calls=%fused_computation.65 | loop fusion | flops 20971520 | bytes 75497480 | tf_op jit(solution)/shard_map/reduce_sum | solution.py:147
  1033.1 40.6 %all-reduce.3 = (f32[]{:T(128)}, f32[]{:T(128)}) all-reduce(f32[]{:T(128)} %get-tuple-element.16, f32[]{:T(128)} %get-tuple-element.15), channel_id=1, replica_groups=mesh['wide'=4,'narrow'=8] {'wide','narrow'}, use_global_device_ids=true, to_apply=%region_2.3 | all-reduce | flops 2 | bytes 16 | tf_op jit(solution)/shard_map/psum | solution.py:146
  1075.0 11.6 multiply_subtract_fusion
  1086.6 13.0 fusion.127
  1099.7 8.7 copy.102
  1108.3 97.8 %all_to_all.146 = f32[128,64,256]{0,1,2:T(8,128)S(1)} all-to-all(f32[128,64,256]{0,1,2:T(8,128)} %copy.102), channel_id=1, replica_groups=mesh['wide'=4,'narrow'=8] {'narrow'}, dimensions={2} | all-to-all | bytes 16777216 | tf_op jit(solution)/shard_map/all_to_all | solution.py:98
  1210.9 29.1 %fusion.46 = f32[128,512,32]{0,1,2:T(8,128)S(1)} fusion(f32[128,512,32]{0,2,1:T(8,128)S(1)} %bitcast.112, s32[512]{0:T(512)S(1)} %multiply_add_fusion.2, f32[512]{0:T(512)S(1)} %broadcast_select_fusion), kind=kOutput, calls=%fused_computation.93 | convolution fusion | flops 12888834048 | bytes 16781312 | tf_op jit(solution)/shard_map/xnz,mn->xmz/dot_general | solution.py:59
  1244.9 186.4 %all_to_all.147 = f32[128,512,32]{0,2,1:T(8,128)} all-to-all(f32[128,512,32]{0,2,1:T(8,128)S(1)} %copy.107), channel_id=1, replica_groups=mesh['wide'=4,'narrow'=8] {'wide'}, dimensions={1} | all-to-all | bytes 16777216 | tf_op jit(solution)/shard_map/all_to_all | solution.py:104
  1431.3 9.9 copy.132
  1441.2 22.5 %fusion.59 = f32[512,128,32]{1,0,2:T(8,128)S(1)} fusion(f32[512,128,32]{1,0,2:T(8,128)} %bitcast.110, s32[512]{0:T(512)S(1)} %multiply_add_fusion.2, f32[512]{0:T(512)S(1)} %broadcast_select_fusion), kind=kOutput, calls=%fused_computation.108 | convolution fusion | flops 12888834048 | bytes 16781312 | tf_op jit(solution)/shard_map/nyz,mn->myz/dot_general | solution.py:59
  1463.7 20.1 %fusion.25 = f32[512,128,32]{1,0,2:T(8,128)S(1)} fusion(f32[512,128,32]{1,0,2:T(8,128)S(1)} %fusion.59, f32[32]{0:T(128)S(1)} %multiply_subtract_fusion.2, f32[512,128]{1,0:T(8,128)S(1)} %broadcast_add_fusion, f32[]{:T(128)S(6)} %div.25, pred[512,128]{1,0:T(8,128)(4,1)S(1)} %broadcast_and_fusion, pred[32]{0:T(512)(128)(4,1)S(1)} %fusion.157, ...), kind=kOutput, calls=%fused_computation.61 | convolution fusion | flops 12901416960 | bytes 17109156 | tf_op jit(solution)/shard_map/myz,mn->nyz/dot_general | solution.py:59
  1488.7 185.9 %all_to_all.148 = f32[512,128,32]{1,2,0:T(8,128)} all-to-all(f32[512,128,32]{1,2,0:T(8,128)S(1)} %copy.111), channel_id=1, replica_groups=mesh['wide'=4,'narrow'=8] {'wide'}, dimensions={0} | all-to-all | bytes 16777216 | tf_op jit(solution)/shard_map/all_to_all | solution.py:114
  1674.6 12.2 copy.153
  1686.7 10.3 all_to_all.131
  1697.0 24.9 %convolution_bitcast_fusion = f32[128,512,32]{0,1,2:T(8,128)S(1)} fusion(f32[128,512,32]{1,0,2:T(8,128)} %all_to_all.131, s32[512]{0:T(512)S(1)} %multiply_add_fusion.2, f32[512]{0:T(512)S(1)} %broadcast_select_fusion), kind=kOutput, calls=%fused_computation.94 | convolution fusion | flops 12888834048 | bytes 16781312 | tf_op jit(solution)/shard_map/xmz,mn->xnz/dot_general | solution.py:59
  1735.1 11.6 copy.117
  1746.7 82.4 %all-to-all-done.7 = f32[128,512,32]{0,2,1:T(8,128)} async-done(((f32[128,512,32]{0,2,1:T(8,128)}), f32[128,512,32]{0,2,1:T(8,128)}, u32[]{:S(2)}, u32[]{:S(2)}) %all-to-all-start.7) | async-done | bytes 8388640 | tf_op jit(solution)/shard_map/all_to_all | solution.py:117
  1833.6 21.2 %multiply_reduce_fusion = (f32[]{:T(128)}, f32[128,64,256]{2,0,1:T(8,128)}) fusion(f32[128,64,256]{2,0,1:T(8,128)} %multiply_subtract_fusion, f32[128,64,256]{0,2,1:T(8,128)S(1)} %bitcast.113, s32[256]{0:T(256)S(1)} %multiply_add_fusion.3, f32[256]{0:T(256)S(1)} %compare_select_fusion), kind=kOutput, calls=%fused_computation.60 | convolution fusion | flops 6447628288 | bytes 25167876 | tf_op jit(solution)/shard_map/xym,mn->xyn/dot_general | solution.py:59
  1854.8 38.1 %psum.23 = f32[]{:T(128)} all-reduce(f32[]{:T(128)} %get-tuple-element.62), channel_id=1, replica_groups=mesh['wide'=4,'narrow'=8] {'wide','narrow'}, use_global_device_ids=true, to_apply=%region_6.7 | all-reduce | flops 1 | bytes 8 | tf_op jit(solution)/shard_map/psum | solution.py:152
  1894.1 13.9 multiply_add_fusion
  1908.0 11.6 copy.118
  (60 shorter events, 119.8 us)
Async XLA Ops:
  2.4 8.4 copy-start.2
  39.8 9.1 collective-permute-start
  44.7 11.2 copy-start.4
  44.7 8.3 collective-permute-start.1
  53.1 3.4 collective-permute-start.2
  54.6 5.4 collective-permute-start.3
  92.6 6.1 copy-start.1
  221.6 104.3 %all-to-all-start = ((f32[128,64,256]{0,1,2:T(8,128)}), f32[128,64,256]{0,1,2:T(8,128)}, u32[]{:S(2)}, u32[]{:S(2)}) async-start(f32[128,64,256]{0,1,2:T(8,128)} %copy.87), calls=%async_computation | async-start | bytes 16777216 | tf_op jit(solution)/shard_map/all_to_all | solution.py:98
  371.5 5.8 copy-start.3
  371.5 186.6 %all-to-all-start.1 = ((f32[128,512,32]{0,2,1:T(8,128)}), f32[128,512,32]{0,2,1:T(8,128)}, u32[]{:S(2)}, u32[]{:S(2)}) async-start(f32[128,512,32]{0,2,1:T(8,128)} %copy.92), calls=%async_computation.1 | async-start | bytes 16777216 | tf_op jit(solution)/shard_map/all_to_all | solution.py:104
  974.9 33.0 %copy-start = (f32[128,64,256]{2,0,1:T(8,128)}, f32[128,64,256]{2,0,1:T(8,128)S(1)}, u32[]{:S(2)}) copy-start(f32[128,64,256]{2,0,1:T(8,128)S(1)} %fusion.129) | copy-start | bytes 25165828
  975.1 14.2 collective-permute-start.5
  977.2 12.1 collective-permute-start.4
  989.3 11.6 collective-permute-start.6
  990.6 10.3 collective-permute-start.7
  1730.1 99.0 %all-to-all-start.7 = ((f32[128,512,32]{0,2,1:T(8,128)}), f32[128,512,32]{0,2,1:T(8,128)}, u32[]{:S(2)}, u32[]{:S(2)}) async-start(f32[128,512,32]{0,2,1:T(8,128)} %copy.113), calls=%async_computation.7 | async-start | bytes 16777216 | tf_op jit(solution)/shard_map/all_to_all | solution.py:117
where the time goes:
time: 1940 us; the launch traced here: 1930 us
  blocking collectives  834 us (43%)
  waiting for transfers between devices  366 us (19%)
  matrix products  259 us (13%)
  other arithmetic  217 us (11%)
  local copies, waits for them, and re-layouts  210 us (11%)
  starting transfers between devices  37.6 us (2%)
    all_to_all x2, blocking collectives, precondition(): lax.all_to_all(spectral, 'wide', split_axis=0, concat_axis=1, tiled=True)  373 us
    dot_general x12, matrix products, transform(): return jnp.einsum(einsum_form, values, matrix, precision=HIGHEST)  259 us
    all_to_all x1, blocking collectives, precondition(): lax.all_to_all(spectral, 'wide', split_axis=1, concat_axis=0, tiled=True)  186 us
    all_to_all x1, waiting for transfers between devices, precondition(): lax.all_to_all(spectral, 'wide', split_axis=1, concat_axis=0, tiled=True)  179 us
    all_to_all x1, blocking collectives, precondition(): lax.all_to_all(spectral, 'narrow', split_axis=1, concat_axis=2, tiled=True)  98 us
    all_to_all x1, blocking collectives, precondition(): lax.all_to_all(spectral, 'narrow', split_axis=2, concat_axis=1, tiled=True)  97.8 us
    all_to_all x1, waiting for transfers between devices, precondition(): lax.all_to_all(spectral, 'narrow', split_axis=2, concat_axis=1, tiled=True)  94.1 us
    all_to_all x1, waiting for transfers between devices, precondition(): lax.all_to_all(spectral, 'narrow', split_axis=1, concat_axis=2, tiled=True)  82.4 us
  transfers between devices with their start and end apart: 11, of which 6 were waited for; matrix products, arithmetic and copies ran while one was open for 2% of the time, Pallas kernels for 0%

commit v1 on v0

--- a/solution.py
+++ b/solution.py
@@ -1,3 +1,4 @@
+import functools
 import jax
 import jax.numpy as jnp
 from jax import lax
@@ -10,6 +11,42 @@
 HIGHEST = lax.Precision.HIGHEST
 FORWARD_FORMS = ("nyz,mn->myz", "xnz,mn->xmz", "xyn,mn->xym")
 INVERSE_FORMS = ("myz,mn->nyz", "xmz,mn->xnz", "xym,mn->xyn")
+
+
+def _resolve_rails(x_part, dim_i, chunk):
+    built = x_part.shape
+    t_next = jnp.moveaxis(
+        x_part.reshape(*built[:dim_i], chunk, built[dim_i] // chunk, *built[dim_i + 1 :]), dim_i, 0
+    )
+    return t_next
+
+
+def use_joints(row_data, row_dim):
+    row_data = jnp.moveaxis(row_data, 0, row_dim)
+    seen_now = row_data.shape
+    extra = row_data.reshape(
+        *seen_now[:row_dim], seen_now[row_dim] * seen_now[row_dim + 1], *seen_now[row_dim + 2 :]
+    )
+    return extra
+
+
+def place_pairs_all(vec, group_axis, buf, incoming_x):
+    u_next, aux = (lax.axis_size(group_axis), lax.axis_index(group_axis))
+    z = _resolve_rails(vec, buf, u_next)
+    heap = [z[aux]]
+    for s in range(1, u_next):
+        q_next = z[(aux + s) % u_next]
+        heap.append(
+            lax.ppermute(
+                q_next, group_axis, perm=[(src_i, (src_i + s) % u_next) for src_i in range(u_next)]
+            )
+        )
+    z = jnp.stack(heap, axis=0)[(aux - jnp.arange(u_next)) % u_next]
+    local_now = use_joints(z, incoming_x)
+    return local_now
+
+
+point_rows_on_mesh = functools.partial(place_pairs_all, group_axis="narrow", buf=2, incoming_x=1)
 
 
 def extended(shard, sides, width):
@@ -94,12 +131,7 @@
 def precondition(grid_field, tables, base_cond):
     table_x, table_y, table_z = tables
     spectral = transform(grid_field, table_z, 2, False)
-    spectral = transform(
-        lax.all_to_all(spectral, "narrow", split_axis=2, concat_axis=1, tiled=True),
-        table_y,
-        1,
-        False,
-    )
+    spectral = transform(point_rows_on_mesh(spectral), table_y, 1, False)
     spectral = transform(
         lax.all_to_all(spectral, "wide", split_axis=1, concat_axis=0, tiled=True), table_x, 0, False
     )

time: 1940 us -> 1950 us (level)
  blocking collectives: 834 us -> 739 us
  waiting for transfers between devices: 366 us -> 422 us
  starting transfers between devices: 37.6 us -> 58 us
    ppermute x0 -> x14, waiting for transfers between devices: none -> 147 us  [place_pairs_all(): lax.ppermute(q_next, group_axis, perm=[(src_i, (src_i + s) % u_next) for...]
    all_to_all x1 -> x0, blocking collectives: 97.8 us -> none  [precondition(): lax.all_to_all(spectral, 'narrow', split_axis=2, concat_axis=1, tiled=True)]
    all_to_all x1 -> x0, waiting for transfers between devices: 94.1 us -> none  [precondition(): lax.all_to_all(spectral, 'narrow', split_axis=2, concat_axis=1, tiled=True)]
    ppermute x0 -> x14, starting transfers between devices: none -> 30.8 us  [place_pairs_all(): lax.ppermute(q_next, group_axis, perm=[(src_i, (src_i + s) % u_next) for...]
    unnamed x14 -> x54, local copies, waits for them, and re-layouts: 40.8 us -> 63.7 us
  transfers between devices with their start and end apart: 11 -> 24, of which waited for: 6 -> 14; matrix products, arithmetic and copies ran while one was open for 2% -> 3% of each run, Pallas kernels for 0% -> 0%
where the time goes in v1:
time: 1950 us; the launch traced here: 1940 us
  blocking collectives  739 us (38%)
  waiting for transfers between devices  422 us (22%)
  matrix products  265 us (14%)
  other arithmetic  227 us (12%)
  local copies, waits for them, and re-layouts  225 us (12%)
  starting transfers between devices  58 us (3%)
    all_to_all x2, blocking collectives, precondition(): lax.all_to_all(spectral, 'wide', split_axis=0, concat_axis=1, tiled=True)  375 us
    dot_general x12, matrix products, transform(): return jnp.einsum(einsum_form, values, matrix, precision=HIGHEST)  265 us
    all_to_all x1, blocking collectives, precondition(): lax.all_to_all(spectral, 'wide', split_axis=1, concat_axis=0, tiled=True)  189 us
    all_to_all x1, waiting for transfers between devices, precondition(): lax.all_to_all(spectral, 'wide', split_axis=1, concat_axis=0, tiled=True)  183 us
    ppermute x14, waiting for transfers between devices, place_pairs_all(): lax.ppermute(q_next, group_axis, perm=[(src_i, (src_i + s) % u_next) for...  147 us
    all_to_all x1, blocking collectives, precondition(): lax.all_to_all(spectral, 'narrow', split_axis=1, concat_axis=2, tiled=True)  97.5 us
    all_to_all x1, waiting for transfers between devices, precondition(): lax.all_to_all(spectral, 'narrow', split_axis=1, concat_axis=2, tiled=True)  82.4 us
    unnamed x54, local copies, waits for them, and re-layouts  63.7 us
  transfers between devices with their start and end apart: 24, of which 14 were waited for; matrix products, arithmetic and copies ran while one was open for 3% of the time, Pallas kernels for 0%

profile of v1, /device:TPU:0, one launch (start us, length us, event | category | flops | bytes accessed | tf_op | source)
XLA Modules:
  0.0 1942.2 jit_solution(2127873021242847566)
XLA Ops:
  2.4 8.4 copy.143
  10.9 14.0 add_bitcast_fusion.1
  24.9 14.4 select_add_fusion
  59.7 20.4 %pad_maximum_fusion = f32[3,130,66,256]{3,1,2,0:T(8,128)} fusion(f32[3,130,1,256]{3,1,2,0:T(8,128)S(1)} %collective-permute-done.3, f32[3,1,64,256]{3,1,2,0:T(1,128)S(1)} %collective-permute-done.1, f32[1,128,64,256]{3,1,2,0:T(8,128)} %copy-done.4, f32[1,128,64,256]{3,1,2,0:T(8,128)} %copy-done.2, f32[1,128,64,256]{3,1,2,0:T(8,128)} %bitcast.172, ...), kind=kLoop, calls=%fused_computation.2 | loop fusion | flops 39536640 | bytes 52715520 | tf_op jit(solution)/shard_map/concatenate | solution.py:61
  80.1 11.6 slice_bitcast_fusion.3
  91.6 10.9 slice_bitcast_fusion.1
  108.6 19.1 fusion.4
  127.7 19.2 fusion.8
  146.8 22.0 %fusion.1 = (f32[128,64,257]{2,0,1:T(8,128)}, f32[128,64,257]{2,0,1:T(8,128)}) fusion(f32[128,64,256]{2,0,1:T(8,128)} %slice.300, f32[128,64,256]{2,0,1:T(8,128)} %get-tuple-element.59), kind=kLoop, calls=%fused_computation.10 | loop fusion | flops 12632064 | bytes 33619968 | tf_op jit(solution)/shard_map/mul | solution.py:125
  168.8 41.1 %fusion.14 = f32[128,64,256]{2,0,1:T(8,128)} fusion(f32[128,64,257]{2,0,1:T(8,128)} %get-tuple-element.24, f32[128,65,256]{2,0,1:T(8,128)} %get-tuple-element.22, f32[129,64,256]{2,0,1:T(8,128)} %get-tuple-element.20, f32[128,64,257]{2,0,1:T(8,128)} %get-tuple-element.25, f32[128,65,256]{2,0,1:T(8,128)} %get-tuple-element.23, ...), kind=kLoop, calls=%fused_computation.43 | loop fusion | flops 31457280 | bytes 109051920 | tf_op jit(solution)/shard_map/sub | solution.py:172
  209.9 13.5 fusion.131
  247.9 11.6 collective-permute-start.8
  267.1 34.0 %collective-permute-done.6 = f32[128,64,32]{0,2,1:T(8,128)} collective-permute-done((f32[128,64,32]{0,2,1:T(8,128)}, f32[128,64,32]{0,2,1:T(8,128)}, u32[]{:S(2)}, u32[]{:S(2)}) %collective-permute-start.6) | collective-permute-done | bytes 1048608 | tf_op jit(solution)/shard_map/ppermute | solution.py:40
  307.5 21.2 %collective-permute-done.8 = f32[128,64,32]{0,2,1:T(8,128)S(1)} collective-permute-done((f32[128,64,32]{0,2,1:T(8,128)S(1)}, f32[128,64,32]{0,2,1:T(8,128)S(1)}, u32[]{:S(2)}, u32[]{:S(2)}) %collective-permute-start.8) | collective-permute-done | bytes 1048608 | tf_op jit(solution)/shard_map/ppermute | solution.py:40
  339.7 32.0 %fusion.43 = f32[128,512,32]{0,1,2:T(8,128)S(1)} fusion(f32[128,512,32]{0,2,1:T(8,128)} %bitcast.169, s32[512]{0:T(512)S(1)} %multiply_add_fusion.2, f32[512]{0:T(512)S(1)} %broadcast_select_fusion), kind=kOutput, calls=%fused_computation.94 | convolution fusion | flops 12888834048 | bytes 16781312 | tf_op jit(solution)/shard_map/xnz,mn->xmz/dot_general | solution.py:96
  387.5 182.5 %all-to-all-done = f32[128,512,32]{0,2,1:T(8,128)} async-done(((f32[128,512,32]{0,2,1:T(8,128)}), f32[128,512,32]{0,2,1:T(8,128)}, u32[]{:S(2)}, u32[]{:S(2)}) %all-to-all-start) | async-done | bytes 8388640 | tf_op jit(solution)/shard_map/all_to_all | solution.py:136
  570.0 9.9 copy.117
  579.9 22.7 %fusion.62 = f32[512,128,32]{1,0,2:T(8,128)S(1)} fusion(f32[512,128,32]{1,0,2:T(8,128)} %bitcast.177, s32[512]{0:T(512)S(1)} %multiply_add_fusion.2, f32[512]{0:T(512)S(1)} %broadcast_select_fusion), kind=kOutput, calls=%fused_computation.141 | convolution fusion | flops 12888834048 | bytes 16781312 | tf_op jit(solution)/shard_map/nyz,mn->myz/dot_general | solution.py:96
  602.7 19.9 %fusion.27 = f32[512,128,32]{1,0,2:T(8,128)S(1)} fusion(f32[512,128,32]{1,0,2:T(8,128)S(1)} %fusion.62, f32[32]{0:T(128)S(1)} %multiply_subtract_fusion.2, f32[512,128]{1,0:T(8,128)S(1)} %broadcast_add_fusion, f32[]{:T(128)S(6)} %div.25, pred[512,128]{1,0:T(8,128)(4,1)S(1)} %broadcast_and_fusion, pred[32]{0:T(512)(128)(4,1)S(1)} %fusion.171, ...), kind=kOutput, calls=%fused_computation.69 | convolution fusion | flops 12901416960 | bytes 17109156 | tf_op jit(solution)/shard_map/myz,mn->nyz/dot_general | solution.py:96
  627.5 187.3 %all_to_all.108 = f32[512,128,32]{1,2,0:T(8,128)} all-to-all(f32[512,128,32]{1,2,0:T(8,128)S(1)} %copy.86), channel_id=1, replica_groups=mesh['wide'=4,'narrow'=8] {'wide'}, dimensions={0} | all-to-all | bytes 16777216 | tf_op jit(solution)/shard_map/all_to_all | solution.py:146
  814.8 12.2 copy.142
  826.9 10.3 all_to_all.85
  837.2 24.9 %convolution_bitcast_fusion.1 = f32[128,512,32]{0,1,2:T(8,128)S(1)} fusion(f32[128,512,32]{1,0,2:T(8,128)} %all_to_all.85, s32[512]{0:T(512)S(1)} %multiply_add_fusion.2, f32[512]{0:T(512)S(1)} %broadcast_select_fusion), kind=kOutput, calls=%fused_computation.97 | convolution fusion | flops 12888834048 | bytes 16781312 | tf_op jit(solution)/shard_map/xmz,mn->xnz/dot_general | solution.py:96
  867.0 97.5 %all_to_all.109 = f32[128,512,32]{0,2,1:T(8,128)S(1)} all-to-all(f32[128,512,32]{0,2,1:T(8,128)S(1)} %copy.88), channel_id=1, replica_groups=mesh['wide'=4,'narrow'=8] {'narrow'}, dimensions={1} | all-to-all | bytes 16777216 | tf_op jit(solution)/shard_map/all_to_all | solution.py:149
  968.9 18.2 fusion.129
  990.3 10.8 fusion.3
  1019.9 25.2 %multiply_reduce_fusion.1 = (f32[]{:T(128)}, f32[]{:T(128)}, f32[128,64,256]{2,0,1:T(8,128)}) fusion(f32[128,64,256]{2,0,1:T(8,128)S(1)} %fusion.129, f32[128,64,256]{2,0,1:T(8,128)} %fusion.14, f32[128,64,257]{2,0,1:T(8,128)} %fusion.3, f32[128,65,256]{2,0,1:T(8,128)} %fusion.7, f32[129,64,256]{2,0,1:T(8,128)} %fusion.5), kind=kLoop, calls=%fused_computation.67 | loop fusion | flops 20971520 | bytes 75497480 | tf_op jit(solution)/shard_map/reduce_sum | solution.py:179
  1045.0 40.6 %all-reduce.3 = (f32[]{:T(128)}, f32[]{:T(128)}) all-reduce(f32[]{:T(128)} %get-tuple-element.16, f32[]{:T(128)} %get-tuple-element.15), channel_id=1, replica_groups=mesh['wide'=4,'narrow'=8] {'wide','narrow'}, use_global_device_ids=true, to_apply=%region_2.3 | all-reduce | flops 2 | bytes 16 | tf_op jit(solution)/shard_map/psum | solution.py:178
  1087.0 11.6 multiply_subtract_fusion
  1098.6 13.5 fusion.127
  1119.6 19.6 %collective-permute-done.15 = f32[128,64,32]{0,2,1:T(8,128)S(1)} collective-permute-done((f32[128,64,32]{0,2,1:T(8,128)S(1)}, f32[128,64,32]{0,2,1:T(8,128)S(1)}, u32[]{:S(2)}, u32[]{:S(2)}) %collective-permute-start.15) | collective-permute-done | bytes 1048608 | tf_op jit(solution)/shard_map/ppermute | solution.py:40
  1143.0 41.5 %collective-permute-done.17 = f32[128,64,32]{0,2,1:T(8,128)S(1)} collective-permute-done((f32[128,64,32]{0,2,1:T(8,128)S(1)}, f32[128,64,32]{0,2,1:T(8,128)S(1)}, u32[]{:S(2)}, u32[]{:S(2)}) %collective-permute-start.17) | collective-permute-done | bytes 1048608 | tf_op jit(solution)/shard_map/ppermute | solution.py:40
  1186.6 20.5 %collective-permute-done.19 = f32[128,64,32]{0,2,1:T(8,128)S(1)} collective-permute-done((f32[128,64,32]{0,2,1:T(8,128)S(1)}, f32[128,64,32]{0,2,1:T(8,128)S(1)}, u32[]{:S(2)}, u32[]{:S(2)}) %collective-permute-start.19) | collective-permute-done | bytes 1048608 | tf_op jit(solution)/shard_map/ppermute | solution.py:40
  1218.2 32.0 %fusion.46 = f32[128,512,32]{0,1,2:T(8,128)S(1)} fusion(f32[128,512,32]{0,2,1:T(8,128)} %bitcast.168, s32[512]{0:T(512)S(1)} %multiply_add_fusion.2, f32[512]{0:T(512)S(1)} %broadcast_select_fusion), kind=kOutput, calls=%fused_computation.95 | convolution fusion | flops 12888834048 | bytes 16781312 | tf_op jit(solution)/shard_map/xnz,mn->xmz/dot_general | solution.py:96
  1255.1 188.6 %all_to_all.110 = f32[128,512,32]{0,2,1:T(8,128)} all-to-all(f32[128,512,32]{0,2,1:T(8,128)S(1)} %copy.95), channel_id=1, replica_groups=mesh['wide'=4,'narrow'=8] {'wide'}, dimensions={1} | all-to-all | bytes 16777216 | tf_op jit(solution)/shard_map/all_to_all | solution.py:136
  1443.7 9.9 copy.120
  1453.6 22.5 %fusion.59 = f32[512,128,32]{1,0,2:T(8,128)S(1)} fusion(f32[512,128,32]{1,0,2:T(8,128)} %bitcast.178, s32[512]{0:T(512)S(1)} %multiply_add_fusion.2, f32[512]{0:T(512)S(1)} %broadcast_select_fusion), kind=kOutput, calls=%fused_computation.140 | convolution fusion | flops 12888834048 | bytes 16781312 | tf_op jit(solution)/shard_map/nyz,mn->myz/dot_general | solution.py:96
  1476.2 20.1 %fusion.25 = f32[512,128,32]{1,0,2:T(8,128)S(1)} fusion(f32[512,128,32]{1,0,2:T(8,128)S(1)} %fusion.59, f32[32]{0:T(128)S(1)} %copy-done.15, f32[512,128]{1,0:T(8,128)S(1)} %copy-done.8, f32[]{:T(128)S(6)} %div.25, pred[512,128]{1,0:T(8,128)(4,1)S(1)} %copy-done.10, pred[32]{0:T(512)(128)(4,1)S(1)} %copy-done.17, s32[512]{0:T(512)S(1)} %multiply_add_fusion.2, ...), kind=kOutput, calls=%fused_computation.63 | convolution fusion | flops 12901416960 | bytes 17109156 | tf_op jit(solution)/shard_map/myz,mn->nyz/dot_general | solution.py:96
  1501.1 187.4 %all_to_all.111 = f32[512,128,32]{1,2,0:T(8,128)} all-to-all(f32[512,128,32]{1,2,0:T(8,128)S(1)} %copy.99), channel_id=1, replica_groups=mesh['wide'=4,'narrow'=8] {'wide'}, dimensions={0} | all-to-all | bytes 16777216 | tf_op jit(solution)/shard_map/all_to_all | solution.py:146
  1688.5 12.2 copy.141
  1700.7 10.3 all_to_all.97
  1710.9 24.9 %convolution_bitcast_fusion = f32[128,512,32]{0,1,2:T(8,128)S(1)} fusion(f32[128,512,32]{1,0,2:T(8,128)} %all_to_all.97, s32[512]{0:T(512)S(1)} %multiply_add_fusion.2, f32[512]{0:T(512)S(1)} %broadcast_select_fusion), kind=kOutput, calls=%fused_computation.96 | convolution fusion | flops 12888834048 | bytes 16781312 | tf_op jit(solution)/shard_map/xmz,mn->xnz/dot_general | solution.py:96
  1749.1 11.6 copy.105
  1760.7 82.4 %all-to-all-done.5 = f32[128,512,32]{0,2,1:T(8,128)} async-done(((f32[128,512,32]{0,2,1:T(8,128)}), f32[128,512,32]{0,2,1:T(8,128)}, u32[]{:S(2)}, u32[]{:S(2)}) %all-to-all-start.5) | async-done | bytes 8388640 | tf_op jit(solution)/shard_map/all_to_all | solution.py:149
  1847.5 21.2 %multiply_reduce_fusion = (f32[]{:T(128)}, f32[128,64,256]{2,0,1:T(8,128)}) fusion(f32[128,64,256]{2,0,1:T(8,128)} %multiply_subtract_fusion, f32[128,64,256]{0,2,1:T(8,128)S(1)} %bitcast.179, s32[256]{0:T(256)S(1)} %multiply_add_fusion.3, f32[256]{0:T(256)S(1)} %compare_select_fusion.3), kind=kOutput, calls=%fused_computation.62 | convolution fusion | flops 6447628288 | bytes 25167876 | tf_op jit(solution)/shard_map/xym,mn->xyn/dot_general | solution.py:96
  1868.8 38.1 %psum.23 = f32[]{:T(128)} all-reduce(f32[]{:T(128)} %get-tuple-element.76), channel_id=1, replica_groups=mesh['wide'=4,'narrow'=8] {'wide','narrow'}, use_global_device_ids=true, to_apply=%region_6.7 | all-reduce | flops 1 | bytes 8 | tf_op jit(solution)/shard_map/psum | solution.py:184
  1908.2 13.9 multiply_add_fusion
  1922.1 11.6 copy.106
  (129 shorter events, 188.7 us)
Async XLA Ops:
  2.4 8.4 copy-start.6
  10.8 41.9 %copy-start.3 = (f32[128,64,256]{2,0,1:T(8,128)}, f32[128,64,256]{2,0,1:T(8,128)S(1)}, u32[]{:S(2)}) copy-start(f32[128,64,256]{2,0,1:T(8,128)S(1)} %copy.143) | copy-start | bytes 25165828
  24.9 27.9 %copy-start.2 = (f32[1,128,64,256]{3,1,2,0:T(8,128)}, f32[1,128,64,256]{3,1,2,0:T(8,128)S(1)}, u32[]{:S(2)}) copy-start(f32[1,128,64,256]{3,1,2,0:T(8,128)S(1)} %get-tuple-element.26) | copy-start | bytes 25165828
  39.2 13.5 copy-start.4
  39.5 9.1 collective-permute-start
  44.5 11.3 copy-start.13
  44.5 8.3 collective-permute-start.1
  52.8 3.6 collective-permute-start.2
  54.3 5.4 collective-permute-start.3
  102.5 6.1 copy-start.1
  223.4 3.4 copy-start.5
  229.5 18.4 collective-permute-start.4
  237.3 27.4 %collective-permute-start.5 = (f32[128,64,32]{0,2,1:T(8,128)}, f32[128,64,32]{0,2,1:T(8,128)}, u32[]{:S(2)}, u32[]{:S(2)}) collective-permute-start(f32[128,64,32]{0,2,1:T(8,128)} %get-tuple-element.57), channel_id=1, source_target_pairs={{0,2},{1,3},{2,4},{3,5},{4,6},{5,7},{6,0},{7,1},{8,10},{9,11},{10,... | collective-permute-start | bytes 3145736 | tf_op jit(solution)/shard_map/ppermute | solution.py:40
  238.8 62.3 %collective-permute-start.6 = (f32[128,64,32]{0,2,1:T(8,128)}, f32[128,64,32]{0,2,1:T(8,128)}, u32[]{:S(2)}, u32[]{:S(2)}) collective-permute-start(f32[128,64,32]{0,2,1:T(8,128)} %get-tuple-element.56), channel_id=1, source_target_pairs={{0,3},{1,4},{2,5},{3,6},{4,7},{5,0},{6,1},{7,2},{8,11},{9,12},{10,... | collective-permute-start | bytes 3145736 | tf_op jit(solution)/shard_map/ppermute | solution.py:40
  238.8 93.0 %copy-start.12 = (s32[1024]{0:T(1024)}, s32[1024]{0:T(1024)S(1)}, u32[]{:S(2)}) copy-start(s32[1024]{0:T(1024)S(1)} %pad_clamp_fusion) | copy-start | bytes 12292
  238.8 67.6 %collective-permute-start.7 = (f32[128,64,32]{0,2,1:T(8,128)}, f32[128,64,32]{0,2,1:T(8,128)S(1)}, u32[]{:S(2)}, u32[]{:S(2)}) collective-permute-start(f32[128,64,32]{0,2,1:T(8,128)} %get-tuple-element.55), channel_id=1, source_target_pairs={{0,4},{1,5},{2,6},{3,7},{4,0},{5,1},{6,2},{7,3},{8,12},{9,13},{10,... | collective-permute-start | bytes 3145736 | tf_op jit(solution)/shard_map/ppermute | solution.py:40
  240.2 90.6 %collective-permute-start.10 = (f32[128,64,32]{0,2,1:T(8,128)S(1)}, f32[128,64,32]{0,2,1:T(8,128)S(1)}, u32[]{:S(2)}, u32[]{:S(2)}) collective-permute-start(f32[128,64,32]{0,2,1:T(8,128)S(1)} %get-tuple-element.52), channel_id=1, source_target_pairs={{0,7},{1,0},{2,1},{3,2},{4,3},{5,4},{6,5},{7,6},{8,15},{9,8},{10,9... | collective-permute-start | bytes 3145736 | tf_op jit(solution)/shard_map/ppermute | solution.py:40
  247.9 80.8 %collective-permute-start.8 = (f32[128,64,32]{0,2,1:T(8,128)S(1)}, f32[128,64,32]{0,2,1:T(8,128)S(1)}, u32[]{:S(2)}, u32[]{:S(2)}) collective-permute-start(f32[128,64,32]{0,2,1:T(8,128)S(1)} %get-tuple-element.54), channel_id=1, source_target_pairs={{0,5},{1,6},{2,7},{3,0},{4,1},{5,2},{6,3},{7,4},{8,13},{9,14},{10,... | collective-permute-start | bytes 3145736 | tf_op jit(solution)/shard_map/ppermute | solution.py:40
  264.7 65.1 %collective-permute-start.9 = (f32[128,64,32]{0,2,1:T(8,128)S(1)}, f32[128,64,32]{0,2,1:T(8,128)S(1)}, u32[]{:S(2)}, u32[]{:S(2)}) collective-permute-start(f32[128,64,32]{0,2,1:T(8,128)S(1)} %get-tuple-element.53), channel_id=1, source_target_pairs={{0,6},{1,7},{2,0},{3,1},{4,2},{5,3},{6,4},{7,5},{8,14},{9,15},{10,... | collective-permute-start | bytes 3145736 | tf_op jit(solution)/shard_map/ppermute | solution.py:40
  380.0 5.7 copy-start.11
  380.0 190.0 %all-to-all-start = ((f32[128,512,32]{0,2,1:T(8,128)}), f32[128,512,32]{0,2,1:T(8,128)}, u32[]{:S(2)}, u32[]{:S(2)}) async-start(f32[128,512,32]{0,2,1:T(8,128)} %copy.82), calls=%async_computation | async-start | bytes 16777216 | tf_op jit(solution)/shard_map/all_to_all | solution.py:136
  387.0 215.6 %copy-start.14 = (f32[32]{0:T(128)}, f32[32]{0:T(128)S(1)}, u32[]{:S(2)}) copy-start(f32[32]{0:T(128)S(1)} %multiply_subtract_fusion.2) | copy-start | bytes 388
  387.1 215.6 %copy-start.16 = (pred[32]{0:T(512)(128)(4,1)}, pred[32]{0:T(512)(128)(4,1)S(1)}, u32[]{:S(2)}) copy-start(pred[32]{0:T(512)(128)(4,1)S(1)} %fusion.171) | copy-start | bytes 100
  387.3 215.3 %copy-start.9 = (pred[512,128]{1,0:T(8,128)(4,1)}, pred[512,128]{1,0:T(8,128)(4,1)S(1)}, u32[]{:S(2)}) copy-start(pred[512,128]{1,0:T(8,128)(4,1)S(1)} %broadcast_and_fusion) | copy-start | bytes 196612
  387.5 215.2 %copy-start.7 = (f32[512,128]{1,0:T(8,128)}, f32[512,128]{1,0:T(8,128)S(1)}, u32[]{:S(2)}) copy-start(f32[512,128]{1,0:T(8,128)S(1)} %broadcast_add_fusion) | copy-start | bytes 786436
  987.1 32.8 %copy-start = (f32[128,64,256]{2,0,1:T(8,128)}, f32[128,64,256]{2,0,1:T(8,128)S(1)}, u32[]{:S(2)}) copy-start(f32[128,64,256]{2,0,1:T(8,128)S(1)} %fusion.129) | copy-start | bytes 25165828
  987.2 14.0 collective-permute-start.12
  989.0 12.1 collective-permute-start.11
  1001.2 11.6 collective-permute-start.13
  1002.5 10.3 collective-permute-start.14
  1113.3 25.9 %collective-permute-start.15 = (f32[128,64,32]{0,2,1:T(8,128)S(1)}, f32[128,64,32]{0,2,1:T(8,128)S(1)}, u32[]{:S(2)}, u32[]{:S(2)}) collective-permute-start(f32[128,64,32]{0,2,1:T(8,128)S(1)} %get-tuple-element.49), channel_id=1, source_target_pairs={{0,1},{1,2},{2,3},{3,4},{4,5},{5,6},{6,7},{7,0},{8,9},{9,10},{10,1... | collective-permute-start | bytes 3145736 | tf_op jit(solution)/shard_map/ppermute | solution.py:40
  1113.4 27.0 %collective-permute-start.16 = (f32[128,64,32]{0,2,1:T(8,128)S(1)}, f32[128,64,32]{0,2,1:T(8,128)S(1)}, u32[]{:S(2)}, u32[]{:S(2)}) collective-permute-start(f32[128,64,32]{0,2,1:T(8,128)S(1)} %get-tuple-element.48), channel_id=1, source_target_pairs={{0,2},{1,3},{2,4},{3,5},{4,6},{5,7},{6,0},{7,1},{8,10},{9,11},{10,... | collective-permute-start | bytes 3145736 | tf_op jit(solution)/shard_map/ppermute | solution.py:40
  1115.7 68.9 %collective-permute-start.17 = (f32[128,64,32]{0,2,1:T(8,128)S(1)}, f32[128,64,32]{0,2,1:T(8,128)S(1)}, u32[]{:S(2)}, u32[]{:S(2)}) collective-permute-start(f32[128,64,32]{0,2,1:T(8,128)S(1)} %get-tuple-element.47), channel_id=1, source_target_pairs={{0,3},{1,4},{2,5},{3,6},{4,7},{5,0},{6,1},{7,2},{8,11},{9,12},{10,... | collective-permute-start | bytes 3145736 | tf_op jit(solution)/shard_map/ppermute | solution.py:40
  1117.3 68.3 %collective-permute-start.18 = (f32[128,64,32]{0,2,1:T(8,128)S(1)}, f32[128,64,32]{0,2,1:T(8,128)S(1)}, u32[]{:S(2)}, u32[]{:S(2)}) collective-permute-start(f32[128,64,32]{0,2,1:T(8,128)S(1)} %get-tuple-element.46), channel_id=1, source_target_pairs={{0,4},{1,5},{2,6},{3,7},{4,0},{5,1},{6,2},{7,3},{8,12},{9,13},{10,... | collective-permute-start | bytes 3145736 | tf_op jit(solution)/shard_map/ppermute | solution.py:40
  1118.5 90.7 %collective-permute-start.21 = (f32[128,64,32]{0,2,1:T(8,128)S(1)}, f32[128,64,32]{0,2,1:T(8,128)S(1)}, u32[]{:S(2)}, u32[]{:S(2)}) collective-permute-start(f32[128,64,32]{0,2,1:T(8,128)S(1)} %get-tuple-element.43), channel_id=1, source_target_pairs={{0,7},{1,0},{2,1},{3,2},{4,3},{5,4},{6,5},{7,6},{8,15},{9,8},{10,9... | collective-permute-start | bytes 3145736 | tf_op jit(solution)/shard_map/ppermute | solution.py:40
  1139.2 67.9 %collective-permute-start.19 = (f32[128,64,32]{0,2,1:T(8,128)S(1)}, f32[128,64,32]{0,2,1:T(8,128)S(1)}, u32[]{:S(2)}, u32[]{:S(2)}) collective-permute-start(f32[128,64,32]{0,2,1:T(8,128)S(1)} %get-tuple-element.45), channel_id=1, source_target_pairs={{0,5},{1,6},{2,7},{3,0},{4,1},{5,2},{6,3},{7,4},{8,13},{9,14},{10,... | collective-permute-start | bytes 3145736 | tf_op jit(solution)/shard_map/ppermute | solution.py:40
  1140.4 67.8 %collective-permute-start.20 = (f32[128,64,32]{0,2,1:T(8,128)S(1)}, f32[128,64,32]{0,2,1:T(8,128)S(1)}, u32[]{:S(2)}, u32[]{:S(2)}) collective-permute-start(f32[128,64,32]{0,2,1:T(8,128)S(1)} %get-tuple-element.44), channel_id=1, source_target_pairs={{0,6},{1,7},{2,0},{3,1},{4,2},{5,3},{6,4},{7,5},{8,14},{9,15},{10,... | collective-permute-start | bytes 3145736 | tf_op jit(solution)/shard_map/ppermute | solution.py:40
  1453.6 22.5 %copy-start.8 = (f32[512,128]{1,0:T(8,128)S(1)}, f32[512,128]{1,0:T(8,128)}, u32[]{:S(2)}) copy-start(f32[512,128]{1,0:T(8,128)} %copy-done.7) | copy-start | bytes 786436
  1453.6 22.6 %copy-start.10 = (pred[512,128]{1,0:T(8,128)(4,1)S(1)}, pred[512,128]{1,0:T(8,128)(4,1)}, u32[]{:S(2)}) copy-start(pred[512,128]{1,0:T(8,128)(4,1)} %copy-done.9) | copy-start | bytes 196612
  1453.6 22.6 %copy-start.15 = (f32[32]{0:T(128)S(1)}, f32[32]{0:T(128)}, u32[]{:S(2)}) copy-start(f32[32]{0:T(128)} %copy-done.14) | copy-start | bytes 388
  1453.6 22.6 %copy-start.17 = (pred[32]{0:T(512)(128)(4,1)S(1)}, pred[32]{0:T(512)(128)(4,1)}, u32[]{:S(2)}) copy-start(pred[32]{0:T(512)(128)(4,1)} %copy-done.16) | copy-start | bytes 100
  1744.1 99.0 %all-to-all-start.5 = ((f32[128,512,32]{0,2,1:T(8,128)}), f32[128,512,32]{0,2,1:T(8,128)}, u32[]{:S(2)}, u32[]{:S(2)}) async-start(f32[128,512,32]{0,2,1:T(8,128)} %copy.101), calls=%async_computation.5 | async-start | bytes 16777216 | tf_op jit(solution)/shard_map/all_to_all | solution.py:149
